TPU v7x, 1024 devices: a whole 8x8x8 slice. The times are simulated.
1024 devices in a mesh: island: 16 (over x, y_hi), fsdp: 8 (over y_lo, core), expert: 8 (over z).
Axes of the slice: x: 8, y: 8 (y_hi: 2, y_lo: 4; y = y_hi * 4 + y_lo), z: 8, core: 2. Of those that a mesh axis runs over, the one named last changes fastest.
Arguments:
- outer_gate: bfloat16 [3072, 8192], P(('fsdp', 'island'), 'expert'), may hold values from -6 to 6
- momentum: float32 [3072, 8192], P(('fsdp', 'island'), 'expert'), may hold values from -4 to 4
- pseudo_grad: bfloat16 [16, 3072, 8192], P('island', 'fsdp', 'expert'), may hold values from -4 to 4
- decay_index: int32 [1], replicated, may hold values from 0 to 32
- inner_weights: bfloat16 [2, 3072, 8192], P(None, 'fsdp', 'expert'), may hold values from -6 to 6
- tokens: bfloat16 [16, 2048, 3072], P('island', 'expert', 'fsdp'), may hold values from -6 to 6
- cotangent: bfloat16 [16, 2048, 3072], P('island', 'expert', 'fsdp'), may hold values from -6 to 6
- routes: int32 [16, 2048, 2], P('island', 'expert'), may hold values from 0 to 7, all different within a row; in each aligned block of 256 rows (0 to 255, 256 to 511, ..., all dimensions but the last counted through in order) at most 64 rows name the same one
- route_weight: float32 [16, 2048, 2], P('island', 'expert'), may hold values from 0.1 to 1
Outputs:
- new_gate: bfloat16 [3072, 8192], P(('fsdp', 'island'), 'expert')
- new_momentum: float32 [3072, 8192], P(('fsdp', 'island'), 'expert')
- token_grad: bfloat16 [16, 2048, 3072], P('island', 'expert', 'fsdp')
Inputs may be any that keep to these rules, and one draw needn't show every extreme that they name: `routes`: each token names 2 different experts. Within every aligned block of 256 tokens every expert is named exactly 64 times.
All inputs are finite; a program needn't handle non-finite values.
Results may differ from a plain program's by a relative error of at most 0.013.
Values may be sent and summed in bfloat16 or wider, within the bound.
A program may use at most 32 MiB of HBM per device.

v0:
```python
import math

import jax
import jax.numpy as jnp
from jax import lax
from jax.sharding import PartitionSpec as P

D = 3072
FFW = 8192
EXPERTS = 8
SCHED = 64


beta_outer = 0.9
rate_outer = 0.7
shrink_rate = 0.2


def swiglu_back(pre_gate, pre_up, back_act):
    sigmoid_gate = jax.nn.sigmoid(pre_gate)
    grad_up = back_act * pre_gate * sigmoid_gate
    grad_gate = back_act * pre_up * sigmoid_gate * (1.0 + pre_gate * (1.0 - sigmoid_gate))
    return (grad_gate.astype(jnp.bfloat16), grad_up.astype(jnp.bfloat16))


def local(
    outer_gate,
    momentum,
    pseudo_grad,
    decay_index,
    inner_weights,
    tokens,
    cotangent,
    routes,
    route_weight,
):
    tok_rows = tokens.shape[1]
    capacity = tok_rows * routes.shape[2] // EXPERTS
    hidden_dev = outer_gate.shape[1]
    in_scale = D ** (-0.5)
    out_scale = FFW ** (-0.5)
    summed_grad = lax.psum_scatter(
        pseudo_grad[0].astype(jnp.float32).astype(jnp.bfloat16),
        "island",
        scatter_dimension=0,
        tiled=True,
    ).astype(jnp.float32)
    mean_grad = summed_grad / lax.axis_size("island")
    step_value = decay_index.astype(jnp.float32)[0]
    rate_now = rate_outer * 0.5 * (1.0 + jnp.cos(math.pi * step_value / SCHED))
    momentum_new = beta_outer * momentum + mean_grad
    gate_new = (
        (1.0 - shrink_rate * rate_now) * outer_gate.astype(jnp.float32)
        - rate_now * (mean_grad + beta_outer * momentum_new)
    ).astype(jnp.bfloat16)
    gate_rows = lax.all_gather(gate_new, "island", axis=0, tiled=True)
    gate_up = jnp.concatenate([gate_rows, inner_weights[0]], axis=1)
    chosen = routes[0] == 0
    hit = jnp.sum(chosen.astype(jnp.int32), axis=1)
    weight_tok = jnp.sum(jnp.where(chosen, route_weight[0], 0.0), axis=1)
    rank = jnp.cumsum(hit) - hit
    match = (rank[None, :] == jnp.arange(capacity, dtype=jnp.int32)[:, None]) & (hit[None, :] > 0)
    placing = match.astype(jnp.bfloat16)
    slot_weight = jnp.sum(jnp.where(match, weight_tok[None, :], 0.0), axis=1)
    sent_tokens = jnp.dot(placing, tokens[0], preferred_element_type=jnp.float32).astype(
        jnp.bfloat16
    )
    sent_cotangent = (
        jnp.dot(placing, cotangent[0], preferred_element_type=jnp.float32) * slot_weight[:, None]
    ).astype(jnp.bfloat16)
    got_tokens, got_cotangent = (
        lax.all_gather(sent_tokens, "expert", axis=0, tiled=True),
        lax.all_gather(sent_cotangent, "expert", axis=0, tiled=True),
    )
    slot_count = got_tokens.shape[0]
    partial_in = jnp.dot(got_tokens, gate_up, preferred_element_type=jnp.float32)
    partial_back = jnp.dot(got_cotangent, inner_weights[1], preferred_element_type=jnp.float32)
    shares_in, shares_back = (
        lax.psum_scatter(
            partial_in.reshape(slot_count, 2, hidden_dev), "fsdp", scatter_dimension=2, tiled=True
        ),
        lax.psum_scatter(partial_back, "fsdp", scatter_dimension=1, tiled=True),
    )
    gate_share, up_share = swiglu_back(
        in_scale * shares_in[:, 0, :], in_scale * shares_in[:, 1, :], out_scale * shares_back
    )
    grad_gate, grad_up = (
        lax.all_gather(gate_share, "fsdp", axis=1, tiled=True),
        lax.all_gather(up_share, "fsdp", axis=1, tiled=True),
    )
    grad_pair = jnp.concatenate([grad_gate, grad_up], axis=1)
    mine = lax.psum_scatter(
        in_scale
        * lax.dot_general(
            grad_pair, gate_up, (((1,), (1,)), ((), ())), preferred_element_type=jnp.float32
        ),
        "expert",
        scatter_dimension=0,
        tiled=True,
    )
    slot_grads = mine.astype(jnp.bfloat16)
    token_grad = lax.dot_general(
        placing, slot_grads, (((0,), (0,)), ((), ())), preferred_element_type=jnp.float32
    )
    return (gate_new, momentum_new, token_grad.astype(jnp.bfloat16)[None])


def solution(mesh):
    return jax.shard_map(
        local,
        mesh=mesh,
        in_specs=(
            P(("fsdp", "island"), "expert"),
            P(("fsdp", "island"), "expert"),
            P("island", "fsdp", "expert"),
            P(),
            P(None, "fsdp", "expert"),
            P("island", "expert", "fsdp"),
            P("island", "expert", "fsdp"),
            P("island", "expert", None),
            P("island", "expert", None),
        ),
        out_specs=(
            P(("fsdp", "island"), "expert"),
            P(("fsdp", "island"), "expert"),
            P("island", "expert", "fsdp"),
        ),
        check_vma=False,
    )
```

profile of v0, /device:TPU:14, one launch (start us, length us, event | category | flops | bytes accessed | tf_op | source)
XLA Modules:
  0.0 535.8 jit_solution(13923954415452510453)
XLA Ops:
  7.2 0.0 copy-start
  7.2 0.0 reduce-scatter.5.cloned.1.call-start
  7.2 0.7 reduce-scatter.5.cloned.1.call-update
  7.9 0.0 reduce-scatter.7.cloned.1.call-start
  8.0 0.7 convert_reduce_fusion
  8.7 0.3 reduce-window.9
  9.0 0.1 slice.19
  9.1 0.1 slice_reduce_fusion
  9.2 0.7 select_reduce_fusion.1
  9.9 0.1 bitcast_subtract_fusion
  10.0 0.1 select_reduce_fusion
  10.1 0.0 copy-done
  10.1 0.2 fusion.8
  10.3 37.2 %all_gather.15 = bf16[512,384]{1,0:T(8,128)(2,1)S(1)} all-gather(bf16[64,384]{1,0:T(8,128)(2,1)S(1)} %fusion.8), channel_id=1, replica_groups=mesh['island'=16,'fsdp'=8,'expert'=8] {'expert'}, dimensions={0}, use_global_device_ids=true | all-gather | bytes 442368 | tf_op jit(solution)/shard_map/all_gather | solution.py:73
  47.5 0.0 copy-start.1
  47.5 3.3 fusion.10
  50.8 0.0 copy-start.3
  50.8 0.0 copy-start.4
  50.8 0.0 reduce-scatter.7.cloned.1.call-update
  50.8 0.0 reduce-scatter.9.cloned.1.call-start
  51.6 0.0 copy-done.1
  51.6 0.2 convolution_convert_fusion.1
  51.8 25.3 %all_gather.16 = bf16[512,384]{1,0:T(8,128)(2,1)S(1)} all-gather(bf16[64,384]{1,0:T(8,128)(2,1)S(1)} %convolution_convert_fusion.1), channel_id=1, replica_groups=mesh['island'=16,'fsdp'=8,'expert'=8] {'expert'}, dimensions={0}, use_global_device_ids=true | all-gather | bytes 442368 | tf_op jit(solution)/shard_map/all_gather | solution.py:72
  77.1 1.2 slice_bitcast_fusion
  78.3 176.8 %reduce-scatter.5.cloned.1.call-done = bf16[24,1024]{1,0:T(8,128)(2,1)} async-done(((bf16[384,1024]{1,0:T(8,128)(2,1)}), bf16[24,1024]{1,0:T(8,128)(2,1)}) %reduce-scatter.5.cloned.1.call-update) | async-done | bytes 49168 | tf_op jit(solution)/shard_map/reduce_scatter | solution.py:42
  255.1 0.0 copy-done.3
  255.1 0.0 copy-done.4
  255.1 1.5 subtract_convert_fusion
  256.6 0.0 copy-start.2
  256.6 70.3 %all_gather.17 = bf16[384,1024]{1,0:T(8,128)(2,1)S(1)} all-gather(bf16[24,1024]{1,0:T(8,128)(2,1)S(1)} %get-tuple-element.3), channel_id=1, replica_groups=mesh['island'=16,'fsdp'=8,'expert'=8] {'island'}, dimensions={0}, use_global_device_ids=true | all-gather | bytes 835584 | tf_op jit(solution)/shard_map/all_gather | solution.py:56
  326.9 3.3 fusion.9
  330.2 0.0 copy-done.2
  330.2 5.4 %copy.15 = f32[512,2,1024]{2,0,1:T(8,128)} copy(f32[512,2,1024]{0,2,1:T(8,128)} %bitcast.38) | data formatting | bytes 8388608 | tf_op jit(solution)/shard_map/reshape | solution.py:80
  335.6 0.0 reduce-scatter.9.cloned.1.call-update
  335.6 0.0 all-gather.5.cloned.1.call-start
  335.6 0.0 reduce-scatter.7.cloned.1.call-done
  335.7 62.0 %reduce-scatter.9.cloned.1.call-done = f32[512,2,128]{2,0,1:T(8,128)} async-done(((f32[512,2,1024]{2,0,1:T(8,128)}), f32[512,2,128]{2,0,1:T(8,128)}) %reduce-scatter.9.cloned.1.call-update) | async-done | bytes 524304 | tf_op jit(solution)/shard_map/reduce_scatter | solution.py:79
  397.6 2.0 fusion.18
  399.6 0.0 all-gather.5.cloned.1.call-update
  399.6 0.0 all-gather.3.cloned.1.call-start
  399.7 0.5 all-gather.3.cloned.1.call-update
  400.2 0.0 reduce-scatter.11.cloned.1.call-start
  400.3 37.4 %all-gather.5.cloned.1.call-done = bf16[512,1024]{1,0:T(8,128)(2,1)} async-done(((bf16[512,128]{1,0:T(8,128)(2,1)}), bf16[512,1024]{1,0:T(8,128)(2,1)}) %all-gather.5.cloned.1.call-update) | async-done | bytes 1048592 | tf_op jit(solution)/shard_map/all_gather | solution.py:89
  437.7 40.5 %all-gather.3.cloned.1.call-done = bf16[512,1024]{1,0:T(8,128)(2,1)} async-done(((bf16[512,128]{1,0:T(8,128)(2,1)}), bf16[512,1024]{1,0:T(8,128)(2,1)}) %all-gather.3.cloned.1.call-update) | async-done | bytes 1048592 | tf_op jit(solution)/shard_map/all_gather | solution.py:88
  478.2 3.7 fusion.4
  481.9 0.0 reduce-scatter.11.cloned.1.call-update
  481.9 45.2 %reduce-scatter.11.cloned.1.call-done = f32[64,384]{1,0:T(8,128)} async-done(((f32[512,384]{1,0:T(8,128)}), f32[64,384]{1,0:T(8,128)}) %reduce-scatter.11.cloned.1.call-update) | async-done | bytes 98320 | tf_op jit(solution)/shard_map/reduce_scatter | solution.py:92
  527.1 1.8 fusion.7
  (2 shorter events, 0.0 us)
Async XLA Ops:
  7.2 3.0 copy-start
  7.2 248.0 %reduce-scatter.5.cloned.1.call-start = ((), (), s32[]{:S(2)}) async-start(), calls=%async_computation.4 | async-start | bytes 835584 | tf_op jit(solution)/shard_map/reduce_scatter | solution.py:42
  7.9 327.8 %reduce-scatter.7.cloned.1.call-start = ((), (), s32[]{:S(2)}) async-start(), calls=%async_computation.5 | async-start | bytes 2359296 | tf_op jit(solution)/shard_map/reduce_scatter | solution.py:82
  47.5 4.1 copy-start.1
  50.8 204.3 %copy-start.3 = (f32[24,1024]{1,0:T(8,128)S(1)}, f32[24,1024]{1,0:T(8,128)}, u32[]{:S(2)}) copy-start(f32[24,1024]{1,0:T(8,128)} %param.10) | copy-start | bytes 294916
  50.8 204.3 %copy-start.4 = (bf16[24,1024]{1,0:T(8,128)(2,1)S(1)}, bf16[24,1024]{1,0:T(8,128)(2,1)}, u32[]{:S(2)}) copy-start(bf16[24,1024]{1,0:T(8,128)(2,1)} %param.9) | copy-start | bytes 147460
  50.8 346.8 %reduce-scatter.9.cloned.1.call-start = ((), (), s32[]{:S(2)}) async-start(), calls=%async_computation.6 | async-start | bytes 4718592 | tf_op jit(solution)/shard_map/reduce_scatter | solution.py:79
  256.6 73.6 %copy-start.2 = (bf16[24,1024]{1,0:T(8,128)(2,1)}, bf16[24,1024]{1,0:T(8,128)(2,1)S(1)}, u32[]{:S(2)}) copy-start(bf16[24,1024]{1,0:T(8,128)(2,1)S(1)} %get-tuple-element.3) | copy-start | bytes 147460
  335.6 102.1 %all-gather.5.cloned.1.call-start = ((), (), s32[]{:S(2)}) async-start(), calls=%async_computation.8 | async-start | bytes 1179648 | tf_op jit(solution)/shard_map/all_gather | solution.py:89
  399.6 78.5 %all-gather.3.cloned.1.call-start = ((), (), s32[]{:S(2)}) async-start(), calls=%async_computation.7 | async-start | bytes 1179648 | tf_op jit(solution)/shard_map/all_gather | solution.py:88
  400.2 126.9 %reduce-scatter.11.cloned.1.call-start = ((), (), s32[]{:S(2)}) async-start(), calls=%async_computation.9 | async-start | bytes 884736 | tf_op jit(solution)/shard_map/reduce_scatter | solution.py:92
Sparse Core Ops, SparseCore 0:
  13.6 241.4 reduce-scatter.4
  258.6 58.0 reduce-scatter.6
  335.7 61.8 reduce-scatter.8
  400.1 37.5 all-gather.4
  440.7 37.4 all-gather.2
  482.0 45.0 reduce-scatter.10
where the time goes:
time: 536 us
  waiting for transfers between devices  363 us (68%)
  blocking collectives  133 us (25%)
  between operations  14.9 us (3%)
  matrix products  12.4 us (2%)
  local copies, waits for them, and re-layouts  6.81 us (1%)
  other arithmetic  5.4 us (1%)
    reduce_scatter x1, waiting for transfers between devices, local(): lax.psum_scatter(pseudo_grad[0].astype(jnp.float32).astype(jnp.bfloat16),...  177 us
    all_gather x1, blocking collectives, local(): gate_rows = lax.all_gather(gate_new, 'island', axis=0, tiled=True)  70.3 us
    reduce_scatter x1, waiting for transfers between devices, local(): lax.psum_scatter(partial_in.reshape(slot_count, 2, hidden_dev), 'fsdp', s...  62 us
    reduce_scatter x1, waiting for transfers between devices, local(): lax.psum_scatter(in_scale * lax.dot_general(grad_pair, gate_up, (((1,), (...  45.2 us
    all_gather x1, waiting for transfers between devices, local(): lax.all_gather(gate_share, 'fsdp', axis=1, tiled=True)  40.5 us
    all_gather x1, waiting for transfers between devices, local(): lax.all_gather(up_share, 'fsdp', axis=1, tiled=True)  37.4 us
    all_gather x1, blocking collectives, local(): lax.all_gather(sent_cotangent, 'expert', axis=0, tiled=True)  37.2 us
    all_gather x1, blocking collectives, local(): lax.all_gather(sent_tokens, 'expert', axis=0, tiled=True)  25.3 us
  transfers between devices with their start and end apart: 6, of which 5 were waited for; matrix products, arithmetic and copies ran while one was open for 3% of the time, Pallas kernels for 0%

commit v1 on v0

v1 whole, which is shorter than its diff:
```python
import functools
import math

import jax
import jax.numpy as jnp
from jax import lax
from jax.experimental import pallas as pl
from jax.experimental.pallas import tpu as pltpu
from jax.sharding import PartitionSpec as P

MESH = pl.DeviceIdType.MESH
BF = jnp.bfloat16
F32 = jnp.float32

D = 3072
FFW = 8192
EXPERTS = 8
SCHED = 64
NX, NYL, NZ = 8, 4, 8
ISL = 16
HALF = 512
QUART = 256
SLOTB = 64
ROWS = 48
FWD = (4, 3)
BWD = (3, 4)

beta_outer = 0.9
rate_outer = 0.7
shrink_rate = 0.2


def kernel(pg, mom, og, dec, inner, tok, cot, routes, rw, o_gate, o_mom, o_tok, *scratch):
    (pv, aR, aL, sf, tw_out, tw_in, gown, gst, gbuf, wbuf, xt, xc, placing, uvp, uvsR, uvsL, uvrR, uvrL, uvf, gp, gsR, gsL,
     grR, grL, agL, agR, sgo, sgs, sgr, zs, zrR, zrL, lsem, a_s, a_r, tw_s, tw_r, pc_s, pc_r, x_s, x_r, w_s, w_r, b_s, b_r,
     bs_s, bs_r, uv_s, uv_r, g_s, g_r, ag_s, ag_r, sb_s, sb_r, z_s, z_r) = scratch
    i = lax.axis_index("island")
    f = lax.axis_index("fsdp")
    z = lax.axis_index("expert")
    x, yh = i // 2, i % 2
    yl, c = f // 2, f % 2
    oc = 1 - c

    def dev(dx=0, twin=False, dyl=0, sib=False, dz=0):
        xx = (x + dx + NX) % NX if dx else x
        yy = 1 - yh if twin else yh
        ll = jnp.clip(yl + dyl, 0, NYL - 1) if dyl else yl
        cc = oc if sib else c
        zz = (z + dz + NZ) % NZ if dz else z
        return (xx * 2 + yy, ll * 2 + cc, zz)

    SIB = dev(sib=True)
    TWIN = dev(twin=True)
    TWSIB = dev(twin=True, sib=True)
    XR, XL, ZR, ZL = dev(dx=1), dev(dx=-1), dev(dz=1), dev(dz=-1)
    YR, YL = dev(dyl=1), dev(dyl=-1)

    def rc(src, dst, ss, rs, device):
        return pltpu.make_async_remote_copy(
            src_ref=src, dst_ref=dst, send_sem=ss, recv_sem=rs, device_id=device, device_id_type=MESH)

    sends = []

    def go(src, dst, ss, rs, device):
        cp = rc(src, dst, ss, rs, device)
        cp.start()
        sends.append(cp)

    def got(dst, ss, rs, device):
        rc(dst, dst, ss, rs, device).wait_recv()

    loads = [pltpu.make_async_copy(pg, pv, lsem.at[0])]
    for m in range(2):
        loads.append(pltpu.make_async_copy(
            inner.at[m, :, pl.ds(pl.multiple_of(c * HALF, HALF), HALF)], wbuf.at[m, c], lsem.at[1 + m]))
    for cp in loads:
        cp.start()

    barrier = pltpu.get_barrier_semaphore()
    for device in (XR, XL, ZR, ZL, SIB, TWIN, TWSIB):
        pl.semaphore_signal(barrier, inc=1, device_id=device, device_id_type=MESH)

    @pl.when(yl < NYL - 1)
    def _():
        pl.semaphore_signal(barrier, inc=1, device_id=YR, device_id_type=MESH)

    @pl.when(yl > 0)
    def _():
        pl.semaphore_signal(barrier, inc=1, device_id=YL, device_id_type=MESH)

    pl.semaphore_wait(barrier, 7 + jnp.minimum(yl, 1) + jnp.minimum(NYL - 1 - yl, 1))

    def prow(j):
        return pl.ds(pl.multiple_of(j * ROWS, 16), ROWS)

    def cols(h):
        return pl.ds(h * HALF, HALF)

    def a_step(s):
        for h in range(2):
            for right in (True, False):
                hops = FWD[h] if right else BWD[h]
                if s >= hops:
                    continue
                buf, d0 = (aR, 0) if right else (aL, 1)
                j = (x + hops - s) % NX if right else (x - hops + s + NX) % NX
                q = h * 8 + d0 * 4
                if s == 0:
                    src = pg.at[prow(j), cols(h)]
                else:
                    got(buf.at[h, s - 1], a_s.at[q + s - 1], a_r.at[q + s - 1], XR)
                    total = buf[h, s - 1].astype(F32) + pv[prow(j), cols(h)].astype(F32)
                    buf[h, s - 1] = total.astype(BF)
                    src = buf.at[h, s - 1]
                go(src, buf.at[h, s], a_s.at[q + s], a_r.at[q + s], XR if right else XL)

    a_step(0)

    for m in range(2):
        go(inner.at[m, :, pl.ds(pl.multiple_of(oc * HALF, HALF), HALF)], wbuf.at[m, c], w_s.at[m], w_r.at[m], SIB)

    chosen = routes[...] == 0
    hit = jnp.max(jnp.where(chosen, 1.0, 0.0), axis=0, keepdims=True)
    weight = jnp.sum(jnp.where(chosen, rw[...], 0.0), axis=0, keepdims=True)
    n_tok = hit.shape[1]
    before = (lax.broadcasted_iota(jnp.int32, (n_tok, n_tok), 0)
              < lax.broadcasted_iota(jnp.int32, (n_tok, n_tok), 1))
    rank = jnp.dot(jnp.broadcast_to(hit, (16, n_tok)).astype(BF), jnp.where(before, 1.0, 0.0).astype(BF),
                   preferred_element_type=F32)[0:1, :]
    slot_id = lax.broadcasted_iota(jnp.int32, (SLOTB, n_tok), 0).astype(F32)
    match = jnp.where((slot_id == rank) & (hit > 0.5), 1.0, 0.0)
    slot_weight = jnp.sum(match * weight, axis=1, keepdims=True)
    placing[...] = match.astype(BF)
    xt[z, c] = jnp.dot(placing[...], tok[...], preferred_element_type=F32).astype(BF)
    xc[z, c] = (jnp.dot(placing[...], cot[...], preferred_element_type=F32) * slot_weight).astype(BF)

    XB = (xt, xc)

    def b_sib(m, n, b):
        go(XB[m].at[b, c], XB[m].at[b, c], bs_s.at[m * 8 + n], bs_r.at[m * 8 + n], SIB)

    def b_step(s):
        for m in range(2):
            for right in (True, False):
                hops = FWD[m] if right else BWD[m]
                q = m * 8 + (0 if right else 4)
                if 0 < s <= hops:
                    b = (z - s + NZ) % NZ if right else (z + s) % NZ
                    got(XB[m].at[b, c], b_s.at[q + s - 1], b_r.at[q + s - 1], ZR)
                    b_out = b
                if s < hops:
                    b_out = z if s == 0 else b
                    go(XB[m].at[b_out, c], XB[m].at[b_out, c], b_s.at[q + s], b_r.at[q + s], ZR if right else ZL)
                if 0 < s <= hops:
                    b_sib(m, s if right else FWD[m] + s, b)
            if s == 0:
                b_sib(m, 0, z)

    b_step(0)

    def uv_block(k):
        d = (k + 1) // 2
        return (z - d + NZ) % NZ if (k % 2 == 1) else (z + d) % NZ

    def uv_compute(k):
        b = uv_block(k)
        d = (k + 1) // 2
        for m in range(2):
            if k == 0:
                n = 0
            elif d == 4:
                n = 4 if m == 0 else FWD[1] + 4
            else:
                n = d if k % 2 == 1 else FWD[m] + d
            got(XB[m].at[b, oc], bs_s.at[m * 8 + n], bs_r.at[m * 8 + n], SIB)
        if k == 0:
            for cp in loads[1:]:
                cp.wait()
            for m in range(2):
                got(wbuf.at[m, oc], w_s.at[m], w_r.at[m], SIB)
        for m in range(2):
            uvp[k, m] = (jnp.dot(XB[m][b, 0], wbuf[m, 0], preferred_element_type=F32)
                         + jnp.dot(XB[m][b, 1], wbuf[m, 1], preferred_element_type=F32))

    def uv_right(k, yy):
        part = uvp[k, :, :, QUART:]
        if yy > 0:
            got(uvrR.at[k], uv_s.at[k], uv_r.at[k], YR)
            part = part + uvrR[k].astype(F32)
        if yy < NYL - 1:
            uvsR[k] = part.astype(BF)
            rc(uvsR.at[k], uvrR.at[k], uv_s.at[k], uv_r.at[k], YR).start()
        else:
            uvf[uv_block(k)] = part

    def uv_left(k, yy):
        part = uvp[k, :, :, :QUART]
        if yy < NYL - 1:
            got(uvrL.at[k], uv_s.at[8 + k], uv_r.at[8 + k], YL)
            part = part + uvrL[k].astype(F32)
        if yy > 0:
            uvsL[k] = part.astype(BF)
            rc(uvsL.at[k], uvrL.at[k], uv_s.at[8 + k], uv_r.at[8 + k], YL).start()
        else:
            uvf[uv_block(k)] = part

    def uv_chain(t):
        for yy in range(NYL):
            kr, kl = t - yy, t - (NYL - 1 - yy)

            @pl.when(yl == yy)
            def _():
                for k, side in sorted(((kr, 1), (kl, 0)), reverse=True):
                    if 0 <= k < 8:
                        (uv_right if side else uv_left)(k, yy)

    loads[0].wait()
    a_step(1)
    b_step(1)
    uv_compute(0)
    a_step(2)
    b_step(2)
    uv_compute(1)
    uv_compute(2)
    uv_chain(0)
    a_step(3)
    b_step(3)
    uv_compute(3)
    uv_compute(4)
    uv_chain(1)

    for h in range(2):
        total = pv[prow(x), cols(h)].astype(F32)
        for buf, hops, q in ((aR, FWD[h], h * 8), (aL, BWD[h], h * 8 + 4)):
            got(buf.at[h, hops - 1], a_s.at[q + hops - 1], a_r.at[q + hops - 1], XR)
            total = total + buf[h, hops - 1].astype(F32)
        for half in range(2):
            part = total[half * 24:(half + 1) * 24]
            sf[half, :, h * HALF:(h + 1) * HALF] = part
            tw_out[half, :, h * HALF:(h + 1) * HALF] = part.astype(BF)
    go(tw_out.at[1 - yh], tw_in, tw_s.at[0], tw_r.at[0], TWIN)
    b_step(4)
    uv_compute(5)
    uv_compute(6)
    uv_chain(2)
    uv_compute(7)
    uv_chain(3)

    step_value = jnp.full((8, 128), dec[0], jnp.int32).astype(F32)
    rate = (rate_outer * 0.5 * (1.0 + jnp.cos(math.pi * step_value / SCHED)))[0:1, 0:1]
    got(tw_in, tw_s.at[0], tw_r.at[0], TWIN)
    mean_grad = (sf[yh] + tw_in[...].astype(F32)) * (1.0 / ISL)
    momentum_new = beta_outer * mom[...] + mean_grad
    gate_new = ((1.0 - shrink_rate * rate) * og[...].astype(F32)
                - rate * (mean_grad + beta_outer * momentum_new)).astype(BF)
    gown[0] = gate_new[:, :HALF]
    gown[1] = gate_new[:, HALF:]
    go(gown.at[c], gst.at[yh, c], pc_s.at[0], pc_r.at[0], TWIN)
    go(gown.at[oc], gst.at[yh, c], pc_s.at[1], pc_r.at[1], TWSIB)
    go(gown.at[oc], gst.at[yh, c], pc_s.at[2], pc_r.at[2], SIB)
    gst[yh, c] = gown[c]
    o_gate[...] = gate_new
    o_mom[...] = momentum_new
    uv_chain(4)
    uv_chain(5)
    got(gst.at[1 - yh, c], pc_s.at[0], pc_r.at[0], TWIN)
    got(gst.at[1 - yh, oc], pc_s.at[1], pc_r.at[1], TWSIB)
    got(gst.at[yh, oc], pc_s.at[2], pc_r.at[2], SIB)
    for ff in range(2):
        gbuf[ff, prow(x), :] = jnp.concatenate(
            [gst[0, ff].astype(F32), gst[1, ff].astype(F32)], axis=0).astype(BF)

    def x_step(s):
        for h in range(2):
            for right in (True, False):
                hops = FWD[h] if right else BWD[h]
                q = h * 8 + (0 if right else 4)
                j = (x - s + NX) % NX if right else (x + s) % NX
                here = gbuf.at[h, prow(j), :]
                if 0 < s <= hops:
                    got(here, x_s.at[q + s - 1], x_r.at[q + s - 1], XR)
                if s < hops:
                    go(here, here, x_s.at[q + s], x_r.at[q + s], XR if right else XL)

    for s in range(5):
        x_step(s)
        uv_chain(6 + s)

    in_scale = D ** (-0.5)
    out_scale = FFW ** (-0.5)

    def block_of(k):
        m = 4 - (k + 1) // 2
        sign = 1 - 2 * ((k + 1) % 2)
        return (z + m * sign + NZ) % NZ

    def swiglu(pre, uv):
        pre_gate = in_scale * pre
        pre_up = in_scale * uv[0]
        back = out_scale * uv[1]
        s = jax.nn.sigmoid(pre_gate)
        gu = back * pre_gate * s
        gg = back * pre_up * s * (1.0 + pre_gate * (1.0 - s))
        return gg.astype(BF), gu.astype(BF)

    def go_when(cond, src, dst, ss, rs, device):
        @pl.when(cond)
        def _():
            rc(src, dst, ss, rs, device).start()

    def inside(k):
        return (k >= 0) & (k < 8)

    def g_compute(k):
        b = block_of(k)
        gp[k] = (jnp.dot(xt[b, 0], gbuf[0], preferred_element_type=F32)
                 + jnp.dot(xt[b, 1], gbuf[1], preferred_element_type=F32))

    def g_right(k):
        @pl.when(yl == 0)
        def _():
            gsR[k] = gp[k, :, QUART:].astype(BF)

        @pl.when(yl > 0)
        def _():
            got(grR.at[k], g_s.at[k], g_r.at[k], YR)
            total = gp[k, :, QUART:] + grR[k].astype(F32)

            @pl.when(yl < NYL - 1)
            def _():
                gsR[k] = total.astype(BF)

            @pl.when(yl == NYL - 1)
            def _():
                gg, gu = swiglu(total, uvf[block_of(k)])
                agR[k, 0] = gg
                agR[k, 1] = gu
                rc(agR.at[k], agR.at[k], ag_s.at[k], ag_r.at[k], YL).start()

        go_when(yl < NYL - 1, gsR.at[k], grR.at[k], g_s.at[k], g_r.at[k], YR)

    def g_left(k):
        @pl.when(yl == NYL - 1)
        def _():
            gsL[k] = gp[k, :, :QUART].astype(BF)

        @pl.when(yl < NYL - 1)
        def _():
            got(grL.at[k], g_s.at[8 + k], g_r.at[8 + k], YL)
            total = gp[k, :, :QUART] + grL[k].astype(F32)

            @pl.when(yl > 0)
            def _():
                gsL[k] = total.astype(BF)

            @pl.when(yl == 0)
            def _():
                gg, gu = swiglu(total, uvf[block_of(k)])
                agL[k, 0] = gg
                agL[k, 1] = gu
                rc(agL.at[k], agL.at[k], ag_s.at[8 + k], ag_r.at[8 + k], YR).start()

        go_when(yl > 0, gsL.at[k], grL.at[k], g_s.at[8 + k], g_r.at[8 + k], YL)

    def ag_left_part(k):
        got(agL.at[k], ag_s.at[8 + k], ag_r.at[8 + k], YR)
        go_when(yl < NYL - 1, agL.at[k], agL.at[k], ag_s.at[8 + k], ag_r.at[8 + k], YR)

    def ag_right_part(k):
        got(agR.at[k], ag_s.at[k], ag_r.at[k], YL)
        go_when(yl > 0, agR.at[k], agR.at[k], ag_s.at[k], ag_r.at[k], YL)

    def back(k):
        gg = jnp.concatenate([agL[k, 0], agR[k, 0]], axis=1)
        gu = jnp.concatenate([agL[k, 1], agR[k, 1]], axis=1)
        dims = (((1,), (1,)), ((), ()))

        def part(ff):
            return in_scale * (
                lax.dot_general(gg, gbuf[ff], dims, preferred_element_type=F32)
                + lax.dot_general(gu, wbuf[0, ff], dims, preferred_element_type=F32))

        sgs[k] = part(oc).astype(BF)
        rc(sgs.at[k], sgr.at[k], sb_s.at[k], sb_r.at[k], SIB).start()
        sgo[k] = part(c)

    def z_stage(k):
        got(sgr.at[k], sb_s.at[k], sb_r.at[k], SIB)
        own = sgo[k] + sgr[k].astype(F32)

        @pl.when(k == 0)
        def _():
            zs[k] = own.astype(BF)
            rc(zs.at[k], zrR.at[0], z_s.at[0], z_r.at[0], ZR).start()

        @pl.when((k % 2 == 1) & (k < 7))
        def _():
            s = (k + 1) // 2
            got(zrR.at[s - 1], z_s.at[s - 1], z_r.at[s - 1], ZR)
            zs[k] = (own + zrR[s - 1].astype(F32)).astype(BF)
            rc(zs.at[k], zrR.at[s], z_s.at[s], z_r.at[s], ZR).start()

        @pl.when(k == 2)
        def _():
            zs[k] = own.astype(BF)
            rc(zs.at[k], zrL.at[0], z_s.at[4], z_r.at[4], ZL).start()

        @pl.when((k % 2 == 0) & (k > 2))
        def _():
            s = k // 2 - 1
            got(zrL.at[s - 1], z_s.at[4 + s - 1], z_r.at[4 + s - 1], ZL)
            zs[k] = (own + zrL[s - 1].astype(F32)).astype(BF)
            rc(zs.at[k], zrL.at[s], z_s.at[4 + s], z_r.at[4 + s], ZL).start()

        @pl.when(k == 7)
        def _():
            got(zrR.at[3], z_s.at[3], z_r.at[3], ZR)
            got(zrL.at[2], z_s.at[6], z_r.at[6], ZL)
            slot_grads = (own + zrR[3].astype(F32) + zrL[2].astype(F32)).astype(BF)
            o_tok[...] = lax.dot_general(
                placing[...], slot_grads, (((0,), (0,)), ((), ())), preferred_element_type=F32).astype(BF)

    last = NYL - 1

    def tick(t, carry):
        def stage(k, fn, cond=None):
            ok = inside(k) if cond is None else inside(k) & cond

            @pl.when(ok)
            def _():
                fn(k)

        stage(t, g_compute)
        stage(t - yl, g_right)
        stage(t - (last - yl), g_left)
        stage(t - last - yl, ag_left_part, yl > 0)
        stage(t - last - (last - yl), ag_right_part, yl < last)
        stage(t - 2 * last, back)
        stage(t - 2 * last - 1, z_stage)
        return carry

    lax.fori_loop(0, 8 + 2 * last + 1, tick, None)

    for cp in sends:
        cp.wait_send()

    def drain(k, carry):
        @pl.when(yl < last)
        def _():
            rc(uvsR.at[k], uvrR.at[k], uv_s.at[k], uv_r.at[k], YR).wait_send()
            rc(gsR.at[k], grR.at[k], g_s.at[k], g_r.at[k], YR).wait_send()
            rc(agL.at[k], agL.at[k], ag_s.at[8 + k], ag_r.at[8 + k], YR).wait_send()

        @pl.when(yl > 0)
        def _():
            rc(uvsL.at[k], uvrL.at[k], uv_s.at[8 + k], uv_r.at[8 + k], YL).wait_send()
            rc(gsL.at[k], grL.at[k], g_s.at[8 + k], g_r.at[8 + k], YL).wait_send()
            rc(agR.at[k], agR.at[k], ag_s.at[k], ag_r.at[k], YL).wait_send()

        rc(sgs.at[k], sgr.at[k], sb_s.at[k], sb_r.at[k], SIB).wait_send()

        @pl.when(k < 7)
        def _():
            rc(zs.at[k], zs.at[k], z_s.at[k], z_r.at[k], ZR).wait_send()

        return carry

    lax.fori_loop(0, 8, drain, None)


def local(outer_gate, momentum, pseudo_grad, decay_index, inner_weights, tokens, cotangent, routes, route_weight):
    vmem = pl.BlockSpec(memory_space=pltpu.VMEM)
    hbm = pl.BlockSpec(memory_space=pl.ANY)
    smem = pl.BlockSpec(memory_space=pltpu.SMEM)
    V = pltpu.VMEM
    S = lambda n: pltpu.SemaphoreType.DMA((n,))
    scratch = [
        V((384, 1024), BF), V((2, 4, ROWS, HALF), BF), V((2, 4, ROWS, HALF), BF),
        V((2, 24, 1024), F32), V((2, 24, 1024), BF), V((24, 1024), BF),
        V((2, 24, HALF), BF), V((2, 2, 24, HALF), BF), V((2, 384, HALF), BF),
        V((2, 2, 384, HALF), BF), V((8, 2, SLOTB, 384), BF), V((8, 2, SLOTB, 384), BF),
        V((SLOTB, 256), BF), V((8, 2, SLOTB, HALF), F32),
        V((8, 2, SLOTB, QUART), BF), V((8, 2, SLOTB, QUART), BF), V((8, 2, SLOTB, QUART), BF), V((8, 2, SLOTB, QUART), BF),
        V((8, 2, SLOTB, QUART), F32), V((8, SLOTB, HALF), F32),
        V((8, SLOTB, QUART), BF), V((8, SLOTB, QUART), BF), V((8, SLOTB, QUART), BF), V((8, SLOTB, QUART), BF),
        V((8, 2, SLOTB, QUART), BF), V((8, 2, SLOTB, QUART), BF),
        V((8, SLOTB, 384), F32), V((8, SLOTB, 384), BF), V((8, SLOTB, 384), BF),
        V((8, SLOTB, 384), BF), V((4, SLOTB, 384), BF), V((3, SLOTB, 384), BF),
        S(3), S(16), S(16), S(1), S(1), S(3), S(3), S(16), S(16), S(2), S(2), S(16), S(16), S(16), S(16),
        S(16), S(16), S(16), S(16), S(16), S(16), S(8), S(8), S(7), S(7),
    ]
    new_gate, new_momentum, token_grad = pl.pallas_call(
        kernel,
        out_shape=(
            jax.ShapeDtypeStruct((24, 1024), BF),
            jax.ShapeDtypeStruct((24, 1024), F32),
            jax.ShapeDtypeStruct((256, 384), BF),
        ),
        in_specs=[hbm, vmem, vmem, smem, hbm, vmem, vmem, vmem, vmem],
        out_specs=(vmem, vmem, vmem),
        scratch_shapes=scratch,
        compiler_params=pltpu.CompilerParams(
            collective_id=0, has_side_effects=True, vmem_limit_bytes=48 << 20),
        name="diloco_swiglu",
    )(pseudo_grad[0], momentum, outer_gate, decay_index, inner_weights, tokens[0], cotangent[0], routes[0].T, route_weight[0].T)
    return new_gate, new_momentum, token_grad[None]


def solution(mesh):
    return jax.shard_map(
        local,
        mesh=mesh,
        in_specs=(
            P(("fsdp", "island"), "expert"),
            P(("fsdp", "island"), "expert"),
            P("island", "fsdp", "expert"),
            P(),
            P(None, "fsdp", "expert"),
            P("island", "expert", "fsdp"),
            P("island", "expert", "fsdp"),
            P("island", "expert", None),
            P("island", "expert", None),
        ),
        out_specs=(
            P(("fsdp", "island"), "expert"),
            P(("fsdp", "island"), "expert"),
            P("island", "expert", "fsdp"),
        ),
        check_vma=False,
    )
```

time: 536 us -> 125 us (0.23)
  waiting for transfers between devices: 363 us -> 0 us
  blocking collectives: 133 us -> 0 us
  Pallas kernels: 0 us -> 112 us
  between operations: 14.9 us -> 1.3 us
  matrix products: 12.4 us -> 0 us
  other arithmetic: 5.4 us -> 0 us
    reduce_scatter x4 -> x0, waiting for transfers between devices: 284 us -> none  [the longest x1 177 us: local(): lax.psum_scatter(pseudo_grad[0].astype(jnp.float32).astype(jnp.bfloat16),...]
    all_gather x3 -> x0, blocking collectives: 133 us -> none  [the longest x1 70.3 us: local(): gate_rows = lax.all_gather(gate_new, 'island', axis=0, tiled=True)]
    pallas_call x0 -> x1, Pallas kernels: none -> 112 us  [local(): pl.pallas_call(kernel, out_shape=(jax.ShapeDtypeStruct((24, 1024), BF), j...]
    all_gather x2 -> x0, waiting for transfers between devices: 77.9 us -> none  [the longest x1 40.5 us: local(): lax.all_gather(gate_share, 'fsdp', axis=1, tiled=True)]
    dot_general x6 -> x0, matrix products: 12.4 us -> none  [the longest x1 3.72 us: local(): lax.dot_general(grad_pair, gate_up, (((1,), (1,)), ((), ())), preferred_e...]
    unnamed x10 -> x19, local copies, waits for them, and re-layouts: 0.02 us -> 9.38 us
    reshape x1 -> x0, local copies, waits for them, and re-layouts: 5.41 us -> none  [local(): partial_in.reshape(slot_count, 2, hidden_dev)]
  transfers between devices with their start and end apart: 6 -> 0, of which waited for: 5 -> 0; matrix products, arithmetic and copies ran while one was open for 3% -> 0% of each run, Pallas kernels for 0% -> 0%
where the time goes in v1:
time: 125 us; the launch traced here: 123 us
  Pallas kernels  112 us (90%)
  local copies, waits for them, and re-layouts  9.38 us (8%)
  between operations  1.3 us (1%)
    pallas_call x1, Pallas kernels, local(): pl.pallas_call(kernel, out_shape=(jax.ShapeDtypeStruct((24, 1024), BF), j...  112 us
    unnamed x19, local copies, waits for them, and re-layouts  9.38 us

profile of v1, /device:TPU:14, one launch (start us, length us, event | category | flops | bytes accessed | tf_op | source)
XLA Modules:
  0.0 123.0 jit_solution(767871927755732266)
XLA Ops:
  1.3 0.0 copy-start
  1.3 1.4 %copy-done = bf16[2,384,1024]{2,1,0:T(8,128)(2,1)S(1)} copy-done((bf16[2,384,1024]{2,1,0:T(8,128)(2,1)S(1)}, bf16[2,384,1024]{2,1,0:T(8,128)(2,1)}, u32[]{:S(2)}) %copy-start) | copy-done | bytes 1572888
  2.7 0.0 copy-start.1
  2.7 1.1 copy-done.1
  3.8 0.0 copy-start.2
  3.8 0.9 copy-done.2
  4.7 0.0 copy-start.3
  4.8 0.9 copy-done.3
  5.7 0.0 copy-start.4
  5.7 0.9 copy-done.4
  6.6 0.0 copy-start.5
  6.6 0.8 copy-done.5
  7.4 0.0 copy-start.6
  7.4 0.7 copy-done.6
  8.1 0.0 copy-start.7
  8.1 0.7 copy-done.7
  8.7 112.4 %diloco_swiglu.1 = (bf16[24,1024]{1,0:T(8,128)(2,1)S(1)}, f32[24,1024]{1,0:T(8,128)S(1)}, bf16[256,384]{1,0:T(8,128)(2,1)S(1)}) custom-call(bf16[384,1024]{1,0:T(8,128)(2,1)S(1)} %bitcast.10, f32[24,1024]{1,0:T(8,128)S(1)} %copy-done.4, bf16[24,1024]{1,0:T(8,128)(2,1)S(1)} %copy-done.5, s32[1]{0:T(128)S(6)} %copy.15.dec, bf16[2,384,1024]{2,1,0:T(8,128)(2,1)S(1)} %copy-done, ...), custom_call_target="tpu_custom_call" | custom-call | tf_op jit(solution)/shard_map/diloco_swiglu/pallas_call | solution.py:492
  121.1 0.6 copy.16
  121.7 0.6 copy.17
  122.4 0.7 copy.18
Async XLA Ops:
  1.3 1.4 %copy-start = (bf16[2,384,1024]{2,1,0:T(8,128)(2,1)S(1)}, bf16[2,384,1024]{2,1,0:T(8,128)(2,1)}, u32[]{:S(2)}) copy-start(bf16[2,384,1024]{2,1,0:T(8,128)(2,1)} %inner.1) | copy-start | bytes 4718596
  2.7 1.1 copy-start.1
  3.8 0.9 copy-start.2
  4.7 0.9 copy-start.3
  5.7 0.9 copy-start.4
  6.6 0.8 copy-start.5
  7.4 0.7 copy-start.6
  8.1 0.7 copy-start.7

commit v2 on v1

v2 whole, which is shorter than its diff:
```python
import functools
import math

import jax
import jax.numpy as jnp
from jax import lax
from jax.experimental import pallas as pl
from jax.experimental.pallas import tpu as pltpu
from jax.sharding import PartitionSpec as P

MESH = pl.DeviceIdType.MESH
BF = jnp.bfloat16
F32 = jnp.float32

D = 3072
FFW = 8192
EXPERTS = 8
SCHED = 64
NX, NYL, NZ = 8, 4, 8
ISL = 16
HALF = 512
UVLAG = 2
GLAG = 2
CH = 256
ORDER = (0, 2, 1, 3)
SLOTB = 64
ROWS = 48
FWD = (4, 3)
BWD = (3, 4)

beta_outer = 0.9
rate_outer = 0.7
shrink_rate = 0.2


def kernel(pg, mom_h, og_h, dec, inner, tok_h, cot_h, routes_h, rw_h, o_gate, o_mom, o_tok, *scratch):
    (mom, og, tok, cot, routes, rw, pv, aR, aL, sf, tw_out, tw_in, gown, gst, gbuf, wbuf, xt, xc, placing, uvp, uvsR, uvsL, uvrR, uvrL, gp, gsR, gsL,
     grR, grL, sgo, sgs, sgr, zs, zrR, zrL, lsem, a_s, a_r, tw_s, tw_r, pc_s, pc_r, x_s, x_r, w_s, w_r, b_s, b_r,
     bs_s, bs_r, uv_s, uv_r, g_s, g_r, sb_s, sb_r, z_s, z_r) = scratch
    i = lax.axis_index("island")
    f = lax.axis_index("fsdp")
    z = lax.axis_index("expert")
    x, yh = i // 2, i % 2
    yl, c = f // 2, f % 2
    oc = 1 - c

    def dev(dx=0, twin=False, dyl=0, sib=False, dz=0):
        xx = (x + dx + NX) % NX if dx else x
        yy = 1 - yh if twin else yh
        ll = jnp.clip(yl + dyl, 0, NYL - 1) if dyl else yl
        cc = oc if sib else c
        zz = (z + dz + NZ) % NZ if dz else z
        return (xx * 2 + yy, ll * 2 + cc, zz)

    SIB = dev(sib=True)
    TWIN = dev(twin=True)
    TWSIB = dev(twin=True, sib=True)
    XR, XL, ZR, ZL = dev(dx=1), dev(dx=-1), dev(dz=1), dev(dz=-1)
    YR, YL = dev(dyl=1), dev(dyl=-1)

    def rc(src, dst, ss, rs, device):
        return pltpu.make_async_remote_copy(
            src_ref=src, dst_ref=dst, send_sem=ss, recv_sem=rs, device_id=device, device_id_type=MESH)

    sends = []

    def go(src, dst, ss, rs, device):
        cp = rc(src, dst, ss, rs, device)
        cp.start()
        sends.append(cp)

    def got(dst, ss, rs, device):
        rc(dst, dst, ss, rs, device).wait_recv()

    loads = [pltpu.make_async_copy(pg, pv, lsem.at[0])]
    for m in range(2):
        loads.append(pltpu.make_async_copy(
            inner.at[m, :, pl.ds(pl.multiple_of(c * HALF, HALF), HALF)], wbuf.at[m, c], lsem.at[1 + m]))
    small = [pltpu.make_async_copy(a, b, lsem.at[3 + n]) for n, (a, b) in enumerate(
        ((routes_h, routes), (rw_h, rw), (tok_h, tok), (cot_h, cot), (mom_h, mom), (og_h, og)))]
    for cp in small[:4] + loads + small[4:]:
        cp.start()

    barrier = pltpu.get_barrier_semaphore()
    for device in (XR, XL, ZR, ZL, SIB, TWIN, TWSIB):
        pl.semaphore_signal(barrier, inc=1, device_id=device, device_id_type=MESH)

    @pl.when(yl < NYL - 1)
    def _():
        pl.semaphore_signal(barrier, inc=1, device_id=YR, device_id_type=MESH)

    @pl.when(yl > 0)
    def _():
        pl.semaphore_signal(barrier, inc=1, device_id=YL, device_id_type=MESH)

    pl.semaphore_wait(barrier, 7 + jnp.minimum(yl, 1) + jnp.minimum(NYL - 1 - yl, 1))

    def prow(j):
        return pl.ds(pl.multiple_of(j * ROWS, 16), ROWS)

    def cols(q):
        return pl.ds(q * CH, CH)

    def a_step(s):
        for q in ORDER:
            for right in (True, False):
                hops = FWD[q // 2] if right else BWD[q // 2]
                if s >= hops:
                    continue
                buf, d0 = (aR, 0) if right else (aL, 1)
                j = (x + hops - s) % NX if right else (x - hops + s + NX) % NX
                n = q * 8 + d0 * 4
                if s == 0:
                    src = pg.at[prow(j), cols(q)]
                else:
                    got(buf.at[q, s - 1], a_s.at[n + s - 1], a_r.at[n + s - 1], XR)
                    total = buf[q, s - 1].astype(F32) + pv[prow(j), cols(q)].astype(F32)
                    buf[q, s - 1] = total.astype(BF)
                    src = buf.at[q, s - 1]
                go(src, buf.at[q, s], a_s.at[n + s], a_r.at[n + s], XR if right else XL)

    a_step(0)

    for m in range(2):
        go(inner.at[m, :, pl.ds(pl.multiple_of(oc * HALF, HALF), HALF)], wbuf.at[m, c], w_s.at[m], w_r.at[m], SIB)

    for cp in small[:4]:
        cp.wait()
    chosen = routes[...] == 0
    hit = jnp.max(jnp.where(chosen, 1.0, 0.0), axis=0, keepdims=True)
    weight = jnp.sum(jnp.where(chosen, rw[...], 0.0), axis=0, keepdims=True)
    n_tok = hit.shape[1]
    before = (lax.broadcasted_iota(jnp.int32, (n_tok, n_tok), 0)
              < lax.broadcasted_iota(jnp.int32, (n_tok, n_tok), 1))
    rank = jnp.dot(jnp.broadcast_to(hit, (16, n_tok)).astype(BF), jnp.where(before, 1.0, 0.0).astype(BF),
                   preferred_element_type=F32)[0:1, :]
    slot_id = lax.broadcasted_iota(jnp.int32, (SLOTB, n_tok), 0).astype(F32)
    match = jnp.where((slot_id == rank) & (hit > 0.5), 1.0, 0.0)
    slot_weight = jnp.sum(match * weight, axis=1, keepdims=True)
    placing[...] = match.astype(BF)
    xt[z, c] = jnp.dot(placing[...], tok[...], preferred_element_type=F32).astype(BF)
    xc[z, c] = (jnp.dot(placing[...], cot[...], preferred_element_type=F32) * slot_weight).astype(BF)

    XB = (xt, xc)

    def b_sib(m, n, b):
        go(XB[m].at[b, c], XB[m].at[b, c], bs_s.at[m * 8 + n], bs_r.at[m * 8 + n], SIB)

    def b_step(s):
        for m in range(2):
            for right in (True, False):
                hops = FWD[m] if right else BWD[m]
                q = m * 8 + (0 if right else 4)
                if 0 < s <= hops:
                    b = (z - s + NZ) % NZ if right else (z + s) % NZ
                    got(XB[m].at[b, c], b_s.at[q + s - 1], b_r.at[q + s - 1], ZR)
                    b_out = b
                if s < hops:
                    b_out = z if s == 0 else b
                    go(XB[m].at[b_out, c], XB[m].at[b_out, c], b_s.at[q + s], b_r.at[q + s], ZR if right else ZL)
                if 0 < s <= hops:
                    b_sib(m, s if right else FWD[m] + s, b)
            if s == 0:
                b_sib(m, 0, z)

    b_step(0)

    def uv_block(k):
        d = (k + 1) // 2
        return (z - d + NZ) % NZ if (k % 2 == 1) else (z + d) % NZ

    def uv_compute(k):
        b = uv_block(k)
        d = (k + 1) // 2
        for m in range(2):
            if k == 0:
                n = 0
            elif d == 4:
                n = 4 if m == 0 else FWD[1] + 4
            else:
                n = d if k % 2 == 1 else FWD[m] + d
            got(XB[m].at[b, oc], bs_s.at[m * 8 + n], bs_r.at[m * 8 + n], SIB)
        if k == 0:
            for cp in loads[1:]:
                cp.wait()
            for m in range(2):
                got(wbuf.at[m, oc], w_s.at[m], w_r.at[m], SIB)
        for m in range(2):
            uvp[k, m] = (jnp.dot(XB[m][b, 0], wbuf[m, 0], preferred_element_type=F32)
                         + jnp.dot(XB[m][b, 1], wbuf[m, 1], preferred_element_type=F32))

    last = NYL - 1

    def inside(k):
        return (k >= 0) & (k < 8)

    def chain(k, part, sR, rR, sL, rL, ss, rs, right):
        got_all, out, base, hasin, hasout, to = (
            (rR, sR, 0, yl > 0, yl < last, YR) if right else (rL, sL, 16, yl < last, yl > 0, YL))
        for e in range(2):
            sem = base + 2 * k + e

            @pl.when(inside(k) & hasin)
            def _():
                got(got_all.at[k, e], ss.at[sem], rs.at[sem], to)

            @pl.when(inside(k) & hasout)
            def _():
                out[k, e] = (part[k, e] + got_all[k, e].astype(F32)).astype(BF)
                rc(out.at[k, e], got_all.at[k, e], ss.at[sem], rs.at[sem], to).start()

    def uv_chain(t):
        chain(t - yl * UVLAG, uvp, uvsR, uvrR, uvsL, uvrL, uv_s, uv_r, True)
        chain(t - (last - yl) * UVLAG, uvp, uvsR, uvrR, uvsL, uvrL, uv_s, uv_r, False)

    @pl.when(yl == 0)
    def _():
        uvrR[...] = jnp.zeros_like(uvrR)
        grR[...] = jnp.zeros_like(grR)

    @pl.when(yl == last)
    def _():
        uvrL[...] = jnp.zeros_like(uvrL)
        grL[...] = jnp.zeros_like(grL)

    loads[0].wait()
    a_step(1)
    b_step(1)
    uv_compute(0)
    uv_chain(0)
    a_step(2)
    b_step(2)
    uv_compute(1)
    uv_chain(1)
    uv_compute(2)
    a_step(3)
    b_step(3)
    uv_compute(3)
    uv_chain(2)
    uv_compute(4)

    for q in ORDER:
        total = pv[prow(x), cols(q)].astype(F32)
        for buf, hops, n in ((aR, FWD[q // 2], q * 8), (aL, BWD[q // 2], q * 8 + 4)):
            got(buf.at[q, hops - 1], a_s.at[n + hops - 1], a_r.at[n + hops - 1], XR)
            total = total + buf[q, hops - 1].astype(F32)
        for half in range(2):
            part = total[half * 24:(half + 1) * 24]
            sf[q, half] = part
            tw_out[q, half] = part.astype(BF)
        go(tw_out.at[q, 1 - yh], tw_in.at[q], tw_s.at[q], tw_r.at[q], TWIN)
    b_step(4)
    uv_compute(5)
    uv_chain(3)
    uv_compute(6)
    uv_chain(4)
    uv_compute(7)

    step_value = jnp.full((8, 128), dec[0], jnp.int32).astype(F32)
    rate = (rate_outer * 0.5 * (1.0 + jnp.cos(math.pi * step_value / SCHED)))[0:1, 0:1]
    for cp in small[4:]:
        cp.wait()
    for e in range(2):
        for q in (e, 2 + e):
            where = slice(q * CH, (q + 1) * CH)
            got(tw_in.at[q], tw_s.at[q], tw_r.at[q], TWIN)
            mean_grad = (sf[q, yh] + tw_in[q].astype(F32)) * (1.0 / ISL)
            momentum_new = beta_outer * mom[:, where] + mean_grad
            gate_new = ((1.0 - shrink_rate * rate) * og[:, where].astype(F32)
                        - rate * (mean_grad + beta_outer * momentum_new)).astype(BF)
            gown[q] = gate_new
            o_gate[:, where] = gate_new
            o_mom[:, where] = momentum_new
        go(gown.at[2 * c + e], gst.at[e, yh, c], pc_s.at[3 * e], pc_r.at[3 * e], TWIN)
        go(gown.at[2 * oc + e], gst.at[e, yh, c], pc_s.at[3 * e + 1], pc_r.at[3 * e + 1], TWSIB)
        go(gown.at[2 * oc + e], gst.at[e, yh, c], pc_s.at[3 * e + 2], pc_r.at[3 * e + 2], SIB)
        gst[e, yh, c] = gown[2 * c + e]
    uv_chain(5)

    def x_step(s, e):
        for h in range(2):
            for right in (True, False):
                hops = FWD[h] if right else BWD[h]
                n = (e * 2 + h) * 8 + (0 if right else 4)
                j = (x - s + NX) % NX if right else (x + s) % NX
                here = gbuf.at[e, h, prow(j), :]
                if 0 < s <= hops:
                    got(here, x_s.at[n + s - 1], x_r.at[n + s - 1], XR)
                if s < hops:
                    go(here, here, x_s.at[n + s], x_r.at[n + s], XR if right else XL)

    for e in range(2):
        got(gst.at[e, yh, oc], pc_s.at[3 * e + 2], pc_r.at[3 * e + 2], SIB)
        got(gst.at[e, 1 - yh, c], pc_s.at[3 * e], pc_r.at[3 * e], TWIN)
        got(gst.at[e, 1 - yh, oc], pc_s.at[3 * e + 1], pc_r.at[3 * e + 1], TWSIB)
        for ff in range(2):
            gbuf[e, ff, prow(x), :] = jnp.concatenate(
                [gst[e, 0, ff].astype(F32), gst[e, 1, ff].astype(F32)], axis=0).astype(BF)
        x_step(0, e)
    uv_chain(6)
    for s in range(1, 5):
        for e in range(2):
            x_step(s, e)
        if s < 4:
            uv_chain(6 + s)

    in_scale = D ** (-0.5)
    out_scale = FFW ** (-0.5)

    def block_of(k):
        m = 4 - (k + 1) // 2
        sign = 1 - 2 * ((k + 1) % 2)
        return (z + m * sign + NZ) % NZ

    def swiglu(pre, uv):
        pre_gate = in_scale * pre
        pre_up = in_scale * uv[0]
        back = out_scale * uv[1]
        s = jax.nn.sigmoid(pre_gate)
        gu = back * pre_gate * s
        gg = back * pre_up * s * (1.0 + pre_gate * (1.0 - s))
        return gg.astype(BF), gu.astype(BF)

    def g_compute(k):
        b = block_of(k)
        for e in range(2):
            gp[k, e] = (jnp.dot(xt[b, 0], gbuf[e, 0], preferred_element_type=F32)
                        + jnp.dot(xt[b, 1], gbuf[e, 1], preferred_element_type=F32))

    def back(k):
        u = 7 - k
        dims = (((1,), (1,)), ((), ()))
        grads = []
        for e in range(2):
            where = slice(e * CH, (e + 1) * CH)
            pre = gp[k, e] + grR[k, e].astype(F32) + grL[k, e].astype(F32)
            uv = [uvp[u, m, :, where] + uvrR[u, m, :, where].astype(F32) + uvrL[u, m, :, where].astype(F32) for m in range(2)]
            grads.append(swiglu(pre, uv))

        def part(ff):
            total = 0.0
            for e, (gg, gu) in enumerate(grads):
                total = total + lax.dot_general(gg, gbuf[e, ff], dims, preferred_element_type=F32)
                total = total + lax.dot_general(
                    gu, wbuf[0, ff, :, e * CH:(e + 1) * CH], dims, preferred_element_type=F32)
            return in_scale * total

        sgs[k] = part(oc).astype(BF)
        rc(sgs.at[k], sgr.at[k], sb_s.at[k], sb_r.at[k], SIB).start()
        sgo[k] = part(c)

    def z_stage(k):
        got(sgr.at[k], sb_s.at[k], sb_r.at[k], SIB)
        own = sgo[k] + sgr[k].astype(F32)

        @pl.when(k == 0)
        def _():
            zs[k] = own.astype(BF)
            rc(zs.at[k], zrR.at[0], z_s.at[0], z_r.at[0], ZR).start()

        @pl.when((k % 2 == 1) & (k < 7))
        def _():
            s = (k + 1) // 2
            got(zrR.at[s - 1], z_s.at[s - 1], z_r.at[s - 1], ZR)
            zs[k] = (own + zrR[s - 1].astype(F32)).astype(BF)
            rc(zs.at[k], zrR.at[s], z_s.at[s], z_r.at[s], ZR).start()

        @pl.when(k == 2)
        def _():
            zs[k] = own.astype(BF)
            rc(zs.at[k], zrL.at[0], z_s.at[4], z_r.at[4], ZL).start()

        @pl.when((k % 2 == 0) & (k > 2))
        def _():
            s = k // 2 - 1
            got(zrL.at[s - 1], z_s.at[4 + s - 1], z_r.at[4 + s - 1], ZL)
            zs[k] = (own + zrL[s - 1].astype(F32)).astype(BF)
            rc(zs.at[k], zrL.at[s], z_s.at[4 + s], z_r.at[4 + s], ZL).start()

        @pl.when(k == 7)
        def _():
            got(zrR.at[3], z_s.at[3], z_r.at[3], ZR)
            got(zrL.at[2], z_s.at[6], z_r.at[6], ZL)
            slot_grads = (own + zrR[3].astype(F32) + zrL[2].astype(F32)).astype(BF)
            o_tok[...] = lax.dot_general(
                placing[...], slot_grads, (((0,), (0,)), ((), ())), preferred_element_type=F32).astype(BF)

    def tick(t, carry):
        def stage(k, fn):
            @pl.when(inside(k))
            def _():
                fn(k)

        chain(t - yl * GLAG, gp, gsR, grR, gsL, grL, g_s, g_r, True)
        chain(t - (last - yl) * GLAG, gp, gsR, grR, gsL, grL, g_s, g_r, False)
        uv_chain(t + 10)
        stage(t + 1, g_compute)
        stage(t - last * GLAG, back)
        stage(t - last * GLAG - 1, z_stage)
        return carry

    g_compute(0)
    lax.fori_loop(0, 8 + last * GLAG + 1, tick, None)

    for cp in sends:
        cp.wait_send()

    def drain(k, carry):
        for e in range(2):
            n = 2 * k + e

            @pl.when(yl < last)
            def _():
                rc(uvsR.at[k, e], uvrR.at[k, e], uv_s.at[n], uv_r.at[n], YR).wait_send()
                rc(gsR.at[k, e], grR.at[k, e], g_s.at[n], g_r.at[n], YR).wait_send()

            @pl.when(yl > 0)
            def _():
                rc(uvsL.at[k, e], uvrL.at[k, e], uv_s.at[16 + n], uv_r.at[16 + n], YL).wait_send()
                rc(gsL.at[k, e], grL.at[k, e], g_s.at[16 + n], g_r.at[16 + n], YL).wait_send()

        rc(sgs.at[k], sgr.at[k], sb_s.at[k], sb_r.at[k], SIB).wait_send()

        @pl.when(k < 7)
        def _():
            rc(zs.at[k], zs.at[k], z_s.at[k], z_r.at[k], ZR).wait_send()

        return carry

    lax.fori_loop(0, 8, drain, None)


def local(outer_gate, momentum, pseudo_grad, decay_index, inner_weights, tokens, cotangent, routes, route_weight):
    vmem = pl.BlockSpec(memory_space=pltpu.VMEM)
    hbm = pl.BlockSpec(memory_space=pltpu.HBM)
    smem = pl.BlockSpec(memory_space=pltpu.SMEM)
    V = pltpu.VMEM
    S = lambda n: pltpu.SemaphoreType.DMA((n,))
    scratch = [
        V((24, 1024), F32), V((24, 1024), BF), V((256, 384), BF), V((256, 384), BF), V((2, 256), jnp.int32), V((2, 256), F32),
        V((384, 1024), BF), V((4, 4, ROWS, CH), BF), V((4, 4, ROWS, CH), BF),
        V((4, 2, 24, CH), F32), V((4, 2, 24, CH), BF), V((4, 24, CH), BF),
        V((4, 24, CH), BF), V((2, 2, 2, 24, CH), BF), V((2, 2, 384, CH), BF),
        V((2, 2, 384, HALF), BF), V((8, 2, SLOTB, 384), BF), V((8, 2, SLOTB, 384), BF),
        V((SLOTB, 256), BF), V((8, 2, SLOTB, HALF), F32),
        V((8, 2, SLOTB, HALF), BF), V((8, 2, SLOTB, HALF), BF), V((8, 2, SLOTB, HALF), BF), V((8, 2, SLOTB, HALF), BF),
        V((8, 2, SLOTB, CH), F32),
        V((8, 2, SLOTB, CH), BF), V((8, 2, SLOTB, CH), BF), V((8, 2, SLOTB, CH), BF), V((8, 2, SLOTB, CH), BF),
        V((8, SLOTB, 384), F32), V((8, SLOTB, 384), BF), V((8, SLOTB, 384), BF),
        V((8, SLOTB, 384), BF), V((4, SLOTB, 384), BF), V((3, SLOTB, 384), BF),
        S(9), S(32), S(32), S(4), S(4), S(6), S(6), S(32), S(32), S(2), S(2), S(16), S(16), S(16), S(16),
        S(32), S(32), S(32), S(32), S(8), S(8), S(7), S(7),
    ]
    new_gate, new_momentum, token_grad = pl.pallas_call(
        kernel,
        out_shape=(
            jax.ShapeDtypeStruct((24, 1024), BF),
            jax.ShapeDtypeStruct((24, 1024), F32),
            jax.ShapeDtypeStruct((256, 384), BF),
        ),
        in_specs=[hbm, hbm, hbm, smem, hbm, hbm, hbm, hbm, hbm],
        out_specs=(vmem, vmem, vmem),
        scratch_shapes=scratch,
        compiler_params=pltpu.CompilerParams(
            collective_id=0, has_side_effects=True, vmem_limit_bytes=67_000_000),
        name="diloco_swiglu",
    )(pseudo_grad[0], momentum, outer_gate, decay_index, inner_weights, tokens[0], cotangent[0], routes[0].T, route_weight[0].T)
    return new_gate, new_momentum, token_grad[None]


def solution(mesh):
    return jax.shard_map(
        local,
        mesh=mesh,
        in_specs=(
            P(("fsdp", "island"), "expert"),
            P(("fsdp", "island"), "expert"),
            P("island", "fsdp", "expert"),
            P(),
            P(None, "fsdp", "expert"),
            P("island", "expert", "fsdp"),
            P("island", "expert", "fsdp"),
            P("island", "expert", None),
            P("island", "expert", None),
        ),
        out_specs=(
            P(("fsdp", "island"), "expert"),
            P(("fsdp", "island"), "expert"),
            P("island", "expert", "fsdp"),
        ),
        check_vma=False,
    )
```

time: 125 us -> 104 us (0.83)
  the two profiles are of different devices: /device:TPU:14 before, /device:TPU:2 now
where the time goes in v2:
time: 104 us
  Pallas kernels  97.8 us (94%)
  local copies, waits for them, and re-layouts  4.58 us (4%)
  between operations  1.29 us (1%)
    pallas_call x1, Pallas kernels, local(): pl.pallas_call(kernel, out_shape=(jax.ShapeDtypeStruct((24, 1024), BF), j...  97.8 us
    unnamed x3, local copies, waits for them, and re-layouts  4.58 us

profile of v2, /device:TPU:2, one launch (start us, length us, event | category | flops | bytes accessed | tf_op | source)
XLA Modules:
  0.0 103.7 jit_solution(5127471472835520113)
XLA Ops:
  1.3 97.8 %diloco_swiglu.1 = (bf16[24,1024]{1,0:T(8,128)(2,1)}, f32[24,1024]{1,0:T(8,128)}, bf16[256,384]{1,0:T(8,128)(2,1)}) custom-call(bf16[384,1024]{1,0:T(8,128)(2,1)} %bitcast.10, f32[24,1024]{1,0:T(8,128)} %mom_h.1, bf16[24,1024]{1,0:T(8,128)(2,1)} %og_h.1, s32[1]{0:T(128)S(6)} %copy.15.dec, bf16[2,384,1024]{2,1,0:T(8,128)(2,1)} %inner.1, ...), custom_call_target="tpu_custom_call" | custom-call | tf_op jit(solution)/shard_map/diloco_swiglu/pallas_call | solution.py:454
  99.1 1.4 %copy.16 = bf16[24,1024]{1,0:T(8,128)(2,1)} copy(bf16[24,1024]{1,0:T(8,128)(2,1)} %get-tuple-element.12) | data formatting | bytes 98304
  100.5 1.5 %copy.17 = f32[24,1024]{1,0:T(8,128)} copy(f32[24,1024]{1,0:T(8,128)} %get-tuple-element.13) | data formatting | bytes 196608
  102.1 1.6 %copy.18 = bf16[1,256,384]{2,1,0:T(8,128)(2,1)} copy(bf16[1,256,384]{2,1,0:T(8,128)(2,1)} %bitcast.13) | data formatting | bytes 393216

commit v3 on v2

--- a/solution.py
+++ b/solution.py
@@ -22,7 +22,6 @@
 UVLAG = 2
 GLAG = 2
 CH = 256
-ORDER = (0, 2, 1, 3)
 SLOTB = 64
 ROWS = 48
 FWD = (4, 3)
@@ -34,8 +33,8 @@
 
 
 def kernel(pg, mom_h, og_h, dec, inner, tok_h, cot_h, routes_h, rw_h, o_gate, o_mom, o_tok, *scratch):
-    (mom, og, tok, cot, routes, rw, pv, aR, aL, sf, tw_out, tw_in, gown, gst, gbuf, wbuf, xt, xc, placing, uvp, uvsR, uvsL, uvrR, uvrL, gp, gsR, gsL,
-     grR, grL, sgo, sgs, sgr, zs, zrR, zrL, lsem, a_s, a_r, tw_s, tw_r, pc_s, pc_r, x_s, x_r, w_s, w_r, b_s, b_r,
+    (momb, ogb, tok, cot, routes, rw, pv, aR, aL, sf, tw_out, tw_in, mall, gall, mfin, gfin, gbuf, wbuf, xt, xc, placing, uvp, uvsR, uvsL, uvrR, uvrL, gp, gsR, gsL,
+     grR, grL, sgo, sgs, sgr, zs, zrR, zrL, lsem, a_s, a_r, tw_s, tw_r, pp_s, pp_r, me_s, me_r, of_s, of_r, x_s, x_r, w_s, w_r, b_s, b_r,
      bs_s, bs_r, uv_s, uv_r, g_s, g_r, sb_s, sb_r, z_s, z_r) = scratch
     i = lax.axis_index("island")
     f = lax.axis_index("fsdp")
@@ -56,6 +55,7 @@
     TWIN = dev(twin=True)
     TWSIB = dev(twin=True, sib=True)
     XR, XL, ZR, ZL = dev(dx=1), dev(dx=-1), dev(dz=1), dev(dz=-1)
+    XRS, XLS = dev(dx=1, sib=True), dev(dx=-1, sib=True)
     YR, YL = dev(dyl=1), dev(dyl=-1)
 
     def rc(src, dst, ss, rs, device):
@@ -72,17 +72,20 @@
     def got(dst, ss, rs, device):
         rc(dst, dst, ss, rs, device).wait_recv()
 
-    loads = [pltpu.make_async_copy(pg, pv, lsem.at[0])]
+    def half_cols(half, first=0, size=HALF):
+        return pl.ds(pl.multiple_of(half * HALF + first, CH), size)
+
+    loads = [pltpu.make_async_copy(pg.at[:, half_cols(c)], pv.at[c], lsem.at[0])]
     for m in range(2):
         loads.append(pltpu.make_async_copy(
             inner.at[m, :, pl.ds(pl.multiple_of(c * HALF, HALF), HALF)], wbuf.at[m, c], lsem.at[1 + m]))
     small = [pltpu.make_async_copy(a, b, lsem.at[3 + n]) for n, (a, b) in enumerate(
-        ((routes_h, routes), (rw_h, rw), (tok_h, tok), (cot_h, cot), (mom_h, mom), (og_h, og)))]
+        ((routes_h, routes), (rw_h, rw), (tok_h, tok), (cot_h, cot), (mom_h.at[:, half_cols(c)], momb.at[c, yh]), (og_h.at[:, half_cols(c)], ogb.at[c, yh])))]
     for cp in small[:4] + loads + small[4:]:
         cp.start()
 
     barrier = pltpu.get_barrier_semaphore()
-    for device in (XR, XL, ZR, ZL, SIB, TWIN, TWSIB):
+    for device in (XR, XL, XRS, XLS, ZR, ZL, SIB, TWIN, TWSIB):
         pl.semaphore_signal(barrier, inc=1, device_id=device, device_id_type=MESH)
 
     @pl.when(yl < NYL - 1)
@@ -93,36 +96,42 @@
     def _():
         pl.semaphore_signal(barrier, inc=1, device_id=YL, device_id_type=MESH)
 
-    pl.semaphore_wait(barrier, 7 + jnp.minimum(yl, 1) + jnp.minimum(NYL - 1 - yl, 1))
+    pl.semaphore_wait(barrier, 9 + jnp.minimum(yl, 1) + jnp.minimum(NYL - 1 - yl, 1))
 
     def prow(j):
         return pl.ds(pl.multiple_of(j * ROWS, 16), ROWS)
 
-    def cols(q):
-        return pl.ds(q * CH, CH)
-
     def a_step(s):
-        for q in ORDER:
-            for right in (True, False):
-                hops = FWD[q // 2] if right else BWD[q // 2]
-                if s >= hops:
-                    continue
-                buf, d0 = (aR, 0) if right else (aL, 1)
-                j = (x + hops - s) % NX if right else (x - hops + s + NX) % NX
-                n = q * 8 + d0 * 4
-                if s == 0:
-                    src = pg.at[prow(j), cols(q)]
-                else:
-                    got(buf.at[q, s - 1], a_s.at[n + s - 1], a_r.at[n + s - 1], XR)
-                    total = buf[q, s - 1].astype(F32) + pv[prow(j), cols(q)].astype(F32)
-                    buf[q, s - 1] = total.astype(BF)
-                    src = buf.at[q, s - 1]
-                go(src, buf.at[q, s], a_s.at[n + s], a_r.at[n + s], XR if right else XL)
+        for e in range(2):
+            for ff in range(2):
+                for right in (True, False):
+                    hops = FWD[e] if right else BWD[e]
+                    if s >= hops:
+                        continue
+                    buf, d0 = (aR, 0) if right else (aL, 4)
+                    j = (x + hops - s) % NX if right else (x - hops + s + NX) % NX
+                    if s == 0:
+                        half = oc if ff else c
+                        to = (XRS if right else XLS) if ff else (XR if right else XL)
+                        go(pg.at[prow(j), half_cols(half, e * CH, CH)], buf.at[2 * c + e, 0],
+                           a_s.at[(2 * half + e) * 8 + d0], a_r.at[(2 * c + e) * 8 + d0], to)
+                    else:
+                        q = 2 * ff + e
+                        n = q * 8 + d0 + s
+                        got(buf.at[q, s - 1], a_s.at[n - 1], a_r.at[n - 1], XR)
+                        total = buf[q, s - 1].astype(F32) + pv[ff, prow(j), e * CH:(e + 1) * CH].astype(F32)
+                        buf[q, s - 1] = total.astype(BF)
+                        go(buf.at[q, s - 1], buf.at[q, s], a_s.at[n], a_r.at[n], XR if right else XL)
 
     a_step(0)
+    go(pg.at[:, half_cols(oc)], pv.at[c], pp_s.at[0], pp_r.at[0], SIB)
 
     for m in range(2):
         go(inner.at[m, :, pl.ds(pl.multiple_of(oc * HALF, HALF), HALF)], wbuf.at[m, c], w_s.at[m], w_r.at[m], SIB)
+
+    for n, (half, to) in enumerate(((c, TWIN), (oc, SIB), (oc, TWSIB))):
+        go(mom_h.at[:, half_cols(half)], momb.at[c, yh], me_s.at[2 * n], me_r.at[2 * n], to)
+        go(og_h.at[:, half_cols(half)], ogb.at[c, yh], me_s.at[2 * n + 1], me_r.at[2 * n + 1], to)
 
     for cp in small[:4]:
         cp.wait()
@@ -224,58 +233,66 @@
         grL[...] = jnp.zeros_like(grL)
 
     loads[0].wait()
+    got(pv.at[oc], pp_s.at[0], pp_r.at[0], SIB)
     a_step(1)
     b_step(1)
     uv_compute(0)
     uv_chain(0)
     a_step(2)
+    uv_compute(1)
     b_step(2)
-    uv_compute(1)
     uv_chain(1)
+    a_step(3)
     uv_compute(2)
-    a_step(3)
     b_step(3)
     uv_compute(3)
     uv_chain(2)
+
+    for e in range(2):
+        for ff in range(2):
+            q = 2 * ff + e
+            total = pv[ff, prow(x), e * CH:(e + 1) * CH].astype(F32)
+            for buf, hops, n in ((aR, FWD[e], q * 8), (aL, BWD[e], q * 8 + 4)):
+                got(buf.at[q, hops - 1], a_s.at[n + hops - 1], a_r.at[n + hops - 1], XR)
+                total = total + buf[q, hops - 1].astype(F32)
+            sf[q] = total
+            tw_out[q] = total.astype(BF)
+            go(tw_out.at[q], tw_in.at[q], tw_s.at[q], tw_r.at[q], TWIN)
     uv_compute(4)
-
-    for q in ORDER:
-        total = pv[prow(x), cols(q)].astype(F32)
-        for buf, hops, n in ((aR, FWD[q // 2], q * 8), (aL, BWD[q // 2], q * 8 + 4)):
-            got(buf.at[q, hops - 1], a_s.at[n + hops - 1], a_r.at[n + hops - 1], XR)
-            total = total + buf[q, hops - 1].astype(F32)
-        for half in range(2):
-            part = total[half * 24:(half + 1) * 24]
-            sf[q, half] = part
-            tw_out[q, half] = part.astype(BF)
-        go(tw_out.at[q, 1 - yh], tw_in.at[q], tw_s.at[q], tw_r.at[q], TWIN)
+    uv_compute(5)
     b_step(4)
-    uv_compute(5)
     uv_chain(3)
     uv_compute(6)
-    uv_chain(4)
     uv_compute(7)
 
     step_value = jnp.full((8, 128), dec[0], jnp.int32).astype(F32)
     rate = (rate_outer * 0.5 * (1.0 + jnp.cos(math.pi * step_value / SCHED)))[0:1, 0:1]
     for cp in small[4:]:
         cp.wait()
-    for e in range(2):
-        for q in (e, 2 + e):
-            where = slice(q * CH, (q + 1) * CH)
+    for n, (ff, hh, to) in enumerate(((c, 1 - yh, TWIN), (oc, yh, SIB), (oc, 1 - yh, TWSIB))):
+        got(momb.at[ff, hh], me_s.at[2 * n], me_r.at[2 * n], to)
+        got(ogb.at[ff, hh], me_s.at[2 * n + 1], me_r.at[2 * n + 1], to)
+
+    def outer_step(e):
+        where = slice(e * CH, (e + 1) * CH)
+        for ff in range(2):
+            q = 2 * ff + e
             got(tw_in.at[q], tw_s.at[q], tw_r.at[q], TWIN)
-            mean_grad = (sf[q, yh] + tw_in[q].astype(F32)) * (1.0 / ISL)
-            momentum_new = beta_outer * mom[:, where] + mean_grad
-            gate_new = ((1.0 - shrink_rate * rate) * og[:, where].astype(F32)
-                        - rate * (mean_grad + beta_outer * momentum_new)).astype(BF)
-            gown[q] = gate_new
-            o_gate[:, where] = gate_new
-            o_mom[:, where] = momentum_new
-        go(gown.at[2 * c + e], gst.at[e, yh, c], pc_s.at[3 * e], pc_r.at[3 * e], TWIN)
-        go(gown.at[2 * oc + e], gst.at[e, yh, c], pc_s.at[3 * e + 1], pc_r.at[3 * e + 1], TWSIB)
-        go(gown.at[2 * oc + e], gst.at[e, yh, c], pc_s.at[3 * e + 2], pc_r.at[3 * e + 2], SIB)
-        gst[e, yh, c] = gown[2 * c + e]
-    uv_chain(5)
+            mean_grad = (sf[q] + tw_in[q].astype(F32)) * (1.0 / ISL)
+            old = jnp.concatenate([momb[ff, 0, :, where], momb[ff, 1, :, where]], axis=0)
+            outer = jnp.concatenate([ogb[ff, 0, :, where].astype(F32), ogb[ff, 1, :, where].astype(F32)], axis=0)
+            momentum_new = beta_outer * old + mean_grad
+            gate_new = (1.0 - shrink_rate * rate) * outer - rate * (mean_grad + beta_outer * momentum_new)
+            gbuf[e, ff, prow(x), :] = gate_new.astype(BF)
+            for hh in range(2):
+                mall[q, hh] = momentum_new[hh * 24:(hh + 1) * 24]
+                gall[q, hh] = gate_new[hh * 24:(hh + 1) * 24].astype(BF)
+
+    def hand_out(e):
+        mfin[c, e] = mall[2 * c + e, yh]
+        gfin[c, e] = gall[2 * c + e, yh]
+        go(mall.at[2 * oc + e, yh], mfin.at[c, e], of_s.at[2 * e], of_r.at[2 * e], SIB)
+        go(gall.at[2 * oc + e, yh], gfin.at[c, e], of_s.at[2 * e + 1], of_r.at[2 * e + 1], SIB)
 
     def x_step(s, e):
         for h in range(2):
@@ -290,19 +307,17 @@
                     go(here, here, x_s.at[n + s], x_r.at[n + s], XR if right else XL)
 
     for e in range(2):
-        got(gst.at[e, yh, oc], pc_s.at[3 * e + 2], pc_r.at[3 * e + 2], SIB)
-        got(gst.at[e, 1 - yh, c], pc_s.at[3 * e], pc_r.at[3 * e], TWIN)
-        got(gst.at[e, 1 - yh, oc], pc_s.at[3 * e + 1], pc_r.at[3 * e + 1], TWSIB)
-        for ff in range(2):
-            gbuf[e, ff, prow(x), :] = jnp.concatenate(
-                [gst[e, 0, ff].astype(F32), gst[e, 1, ff].astype(F32)], axis=0).astype(BF)
+        outer_step(e)
         x_step(0, e)
-    uv_chain(6)
+    uv_chain(4)
+    for e in range(2):
+        hand_out(e)
+    uv_chain(5)
     for s in range(1, 5):
         for e in range(2):
             x_step(s, e)
         if s < 4:
-            uv_chain(6 + s)
+            uv_chain(5 + s)
 
     in_scale = D ** (-0.5)
     out_scale = FFW ** (-0.5)
@@ -393,14 +408,22 @@
 
         chain(t - yl * GLAG, gp, gsR, grR, gsL, grL, g_s, g_r, True)
         chain(t - (last - yl) * GLAG, gp, gsR, grR, gsL, grL, g_s, g_r, False)
-        uv_chain(t + 10)
-        stage(t + 1, g_compute)
+        uv_chain(t + 9)
         stage(t - last * GLAG, back)
         stage(t - last * GLAG - 1, z_stage)
+        stage(t + 1, g_compute)
         return carry
 
     g_compute(0)
     lax.fori_loop(0, 8 + last * GLAG + 1, tick, None)
+
+    for e in range(2):
+        got(mfin.at[oc, e], of_s.at[2 * e], of_r.at[2 * e], SIB)
+        got(gfin.at[oc, e], of_s.at[2 * e + 1], of_r.at[2 * e + 1], SIB)
+        for half in range(2):
+            where = slice(half * HALF + e * CH, half * HALF + (e + 1) * CH)
+            o_mom[:, where] = mfin[half, e]
+            o_gate[:, where] = gfin[half, e]
 
     for cp in sends:
         cp.wait_send()
@@ -437,10 +460,10 @@
     V = pltpu.VMEM
     S = lambda n: pltpu.SemaphoreType.DMA((n,))
     scratch = [
-        V((24, 1024), F32), V((24, 1024), BF), V((256, 384), BF), V((256, 384), BF), V((2, 256), jnp.int32), V((2, 256), F32),
-        V((384, 1024), BF), V((4, 4, ROWS, CH), BF), V((4, 4, ROWS, CH), BF),
-        V((4, 2, 24, CH), F32), V((4, 2, 24, CH), BF), V((4, 24, CH), BF),
-        V((4, 24, CH), BF), V((2, 2, 2, 24, CH), BF), V((2, 2, 384, CH), BF),
+        V((2, 2, 24, HALF), F32), V((2, 2, 24, HALF), BF), V((256, 384), BF), V((256, 384), BF), V((2, 256), jnp.int32), V((2, 256), F32),
+        V((2, 384, HALF), BF), V((4, 4, ROWS, CH), BF), V((4, 4, ROWS, CH), BF),
+        V((4, ROWS, CH), F32), V((4, ROWS, CH), BF), V((4, ROWS, CH), BF),
+        V((4, 2, 24, CH), F32), V((4, 2, 24, CH), BF), V((2, 2, 24, CH), F32), V((2, 2, 24, CH), BF), V((2, 2, 384, CH), BF),
         V((2, 2, 384, HALF), BF), V((8, 2, SLOTB, 384), BF), V((8, 2, SLOTB, 384), BF),
         V((SLOTB, 256), BF), V((8, 2, SLOTB, HALF), F32),
         V((8, 2, SLOTB, HALF), BF), V((8, 2, SLOTB, HALF), BF), V((8, 2, SLOTB, HALF), BF), V((8, 2, SLOTB, HALF), BF),
@@ -448,7 +471,7 @@
         V((8, 2, SLOTB, CH), BF), V((8, 2, SLOTB, CH), BF), V((8, 2, SLOTB, CH), BF), V((8, 2, SLOTB, CH), BF),
         V((8, SLOTB, 384), F32), V((8, SLOTB, 384), BF), V((8, SLOTB, 384), BF),
         V((8, SLOTB, 384), BF), V((4, SLOTB, 384), BF), V((3, SLOTB, 384), BF),
-        S(9), S(32), S(32), S(4), S(4), S(6), S(6), S(32), S(32), S(2), S(2), S(16), S(16), S(16), S(16),
+        S(9), S(32), S(32), S(4), S(4), S(1), S(1), S(6), S(6), S(4), S(4), S(32), S(32), S(2), S(2), S(16), S(16), S(16), S(16),
         S(32), S(32), S(32), S(32), S(8), S(8), S(7), S(7),
     ]
     new_gate, new_momentum, token_grad = pl.pallas_call(

time: 104 us -> 99.7 us (0.959)
  the two profiles are of different devices: /device:TPU:2 before, /device:TPU:14 now
where the time goes in v3:
time: 99.7 us; the launch traced here: 99.4 us
  Pallas kernels  93.5 us (94%)
  local copies, waits for them, and re-layouts  4.58 us (5%)
  between operations  1.29 us (1%)
    pallas_call x1, Pallas kernels, local(): pl.pallas_call(kernel, out_shape=(jax.ShapeDtypeStruct((24, 1024), BF), j...  93.5 us
    unnamed x3, local copies, waits for them, and re-layouts  4.58 us

profile of v3, /device:TPU:14, one launch (start us, length us, event | category | flops | bytes accessed | tf_op | source)
XLA Modules:
  0.0 99.4 jit_solution(5346424131826652377)
XLA Ops:
  1.3 93.5 %diloco_swiglu.1 = (bf16[24,1024]{1,0:T(8,128)(2,1)}, f32[24,1024]{1,0:T(8,128)}, bf16[256,384]{1,0:T(8,128)(2,1)}) custom-call(bf16[384,1024]{1,0:T(8,128)(2,1)} %bitcast.10, f32[24,1024]{1,0:T(8,128)} %mom_h.1, bf16[24,1024]{1,0:T(8,128)(2,1)} %og_h.1, s32[1]{0:T(128)S(6)} %copy.15.dec, bf16[2,384,1024]{2,1,0:T(8,128)(2,1)} %inner.1, ...), custom_call_target="tpu_custom_call" | custom-call | tf_op jit(solution)/shard_map/diloco_swiglu/pallas_call | solution.py:477
  94.8 1.4 %copy.16 = bf16[24,1024]{1,0:T(8,128)(2,1)} copy(bf16[24,1024]{1,0:T(8,128)(2,1)} %get-tuple-element.12) | data formatting | bytes 98304
  96.2 1.5 %copy.17 = f32[24,1024]{1,0:T(8,128)} copy(f32[24,1024]{1,0:T(8,128)} %get-tuple-element.13) | data formatting | bytes 196608
  97.8 1.6 %copy.18 = bf16[1,256,384]{2,1,0:T(8,128)(2,1)} copy(bf16[1,256,384]{2,1,0:T(8,128)(2,1)} %bitcast.13) | data formatting | bytes 393216

commit v4 on v3

--- a/solution.py
+++ b/solution.py
@@ -313,11 +313,10 @@
     for e in range(2):
         hand_out(e)
     uv_chain(5)
-    for s in range(1, 5):
+    for s in range(1, 4):
         for e in range(2):
             x_step(s, e)
-        if s < 4:
-            uv_chain(5 + s)
+        uv_chain(5 + s)
 
     in_scale = D ** (-0.5)
     out_scale = FFW ** (-0.5)
@@ -336,9 +335,9 @@
         gg = back * pre_up * s * (1.0 + pre_gate * (1.0 - s))
         return gg.astype(BF), gu.astype(BF)
 
-    def g_compute(k):
+    def g_compute(k, parts=(0, 1)):
         b = block_of(k)
-        for e in range(2):
+        for e in parts:
             gp[k, e] = (jnp.dot(xt[b, 0], gbuf[e, 0], preferred_element_type=F32)
                         + jnp.dot(xt[b, 1], gbuf[e, 1], preferred_element_type=F32))
 
@@ -400,11 +399,27 @@
             o_tok[...] = lax.dot_general(
                 placing[...], slot_grads, (((0,), (0,)), ((), ())), preferred_element_type=F32).astype(BF)
 
+    def finish_early():
+        for e in range(2):
+            got(mfin.at[oc, e], of_s.at[2 * e], of_r.at[2 * e], SIB)
+            got(gfin.at[oc, e], of_s.at[2 * e + 1], of_r.at[2 * e + 1], SIB)
+            for half in range(2):
+                where = slice(half * HALF + e * CH, half * HALF + (e + 1) * CH)
+                o_mom[:, where] = mfin[half, e]
+                o_gate[:, where] = gfin[half, e]
+
+        for cp in sends:
+            cp.wait_send()
+
     def tick(t, carry):
         def stage(k, fn):
             @pl.when(inside(k))
             def _():
                 fn(k)
+
+        @pl.when(t == 4)
+        def _():
+            finish_early()
 
         chain(t - yl * GLAG, gp, gsR, grR, gsL, grL, g_s, g_r, True)
         chain(t - (last - yl) * GLAG, gp, gsR, grR, gsL, grL, g_s, g_r, False)
@@ -414,19 +429,10 @@
         stage(t + 1, g_compute)
         return carry
 
-    g_compute(0)
+    for e in range(2):
+        x_step(4, e)
+        g_compute(0, (e,))
     lax.fori_loop(0, 8 + last * GLAG + 1, tick, None)
-
-    for e in range(2):
-        got(mfin.at[oc, e], of_s.at[2 * e], of_r.at[2 * e], SIB)
-        got(gfin.at[oc, e], of_s.at[2 * e + 1], of_r.at[2 * e + 1], SIB)
-        for half in range(2):
-            where = slice(half * HALF + e * CH, half * HALF + (e + 1) * CH)
-            o_mom[:, where] = mfin[half, e]
-            o_gate[:, where] = gfin[half, e]
-
-    for cp in sends:
-        cp.wait_send()
 
     def drain(k, carry):
         for e in range(2):
@@ -451,6 +457,14 @@
         return carry
 
     lax.fori_loop(0, 8, drain, None)
+
+
+def write_out(a, b, c, oa, ob, oc, sem):
+    copies = [pltpu.make_async_copy(src, dst, sem.at[n]) for n, (src, dst) in enumerate(((a, oa), (b, ob), (c, oc)))]
+    for cp in copies:
+        cp.start()
+    for cp in copies:
+        cp.wait()
 
 
 def local(outer_gate, momentum, pseudo_grad, decay_index, inner_weights, tokens, cotangent, routes, route_weight):
@@ -488,6 +502,14 @@
             collective_id=0, has_side_effects=True, vmem_limit_bytes=67_000_000),
         name="diloco_swiglu",
     )(pseudo_grad[0], momentum, outer_gate, decay_index, inner_weights, tokens[0], cotangent[0], routes[0].T, route_weight[0].T)
+    new_gate, new_momentum, token_grad = pl.pallas_call(
+        write_out,
+        out_shape=tuple(jax.ShapeDtypeStruct(a.shape, a.dtype) for a in (new_gate, new_momentum, token_grad)),
+        in_specs=[vmem, vmem, vmem],
+        out_specs=(hbm, hbm, hbm),
+        scratch_shapes=[S(3)],
+        name="write_out",
+    )(new_gate, new_momentum, token_grad)
     return new_gate, new_momentum, token_grad[None]
 
 

time: 99.7 us -> 96.7 us (0.970)
  local copies, waits for them, and re-layouts: 4.58 us -> 0 us
  Pallas kernels: 93.5 us -> 95.1 us
    unnamed x3 -> x0, local copies, waits for them, and re-layouts: 4.58 us -> none
    pallas_call x0 -> x1, Pallas kernels: none -> 1.75 us  [local(): pl.pallas_call(write_out, out_shape=tuple((jax.ShapeDtypeStruct(a.shape,...]
where the time goes in v4:
time: 96.7 us; the launch traced here: 96.4 us
  Pallas kernels  95.1 us (98%)
  between operations  1.29 us (1%)
    pallas_call x1, Pallas kernels, local(): pl.pallas_call(kernel, out_shape=(jax.ShapeDtypeStruct((24, 1024), BF), j...  93.3 us

profile of v4, /device:TPU:14, one launch (start us, length us, event | category | flops | bytes accessed | tf_op | source)
XLA Modules:
  0.0 96.4 jit_solution(15125556830086658984)
XLA Ops:
  1.3 93.3 %diloco_swiglu.1 = (bf16[24,1024]{1,0:T(8,128)(2,1)}, f32[24,1024]{1,0:T(8,128)}, bf16[256,384]{1,0:T(8,128)(2,1)}) custom-call(bf16[384,1024]{1,0:T(8,128)(2,1)} %bitcast.10, f32[24,1024]{1,0:T(8,128)} %mom_h.1, bf16[24,1024]{1,0:T(8,128)(2,1)} %og_h.1, s32[1]{0:T(128)S(6)} %copy.12.dec, bf16[2,384,1024]{2,1,0:T(8,128)(2,1)} %inner.1, ...), custom_call_target="tpu_custom_call" | custom-call | tf_op jit(solution)/shard_map/diloco_swiglu/pallas_call | solution.py:491
  94.6 1.8 %write_out.1 = (bf16[24,1024]{1,0:T(8,128)(2,1)}, f32[24,1024]{1,0:T(8,128)}, bf16[256,384]{1,0:T(8,128)(2,1)}) custom-call(bf16[24,1024]{1,0:T(8,128)(2,1)} %get-tuple-element.9.a, f32[24,1024]{1,0:T(8,128)} %get-tuple-element.10.b, bf16[256,384]{1,0:T(8,128)(2,1)} %get-tuple-element.11.c), custom_call_target="tpu_custom_call" | custom-call | tf_op jit(solution)/shard_map/write_out/pallas_call | solution.py:505
